TPU v7x, 256 devices: a whole 4x4x8 slice. The times are simulated.
256 devices in a mesh: shard: 16 (over z, core), tensor: 4 (over x), section: 4 (over y).
Axes of the slice: x: 4, y: 4, z: 8, core: 2. Of those that a mesh axis runs over, the one named last changes fastest.
Arguments:
- gradient: bfloat16 [6, 2048, 8192], P(None, ('tensor', 'section'), 'shard'), may hold values from -6 to 6
- basis: bfloat16 [6, 2048, 256], P(None, ('tensor', 'section')), may hold values from -6 to 6
- moment_m: float32 [6, 8192, 256], P(None, ('shard', 'tensor', 'section')), may hold values from -4 to 4
- moment_v: float32 [6, 8192, 256], P(None, ('shard', 'tensor', 'section')), may hold values from 0.002 to 0.02
Outputs:
- delta: bfloat16 [6, 2048, 8192], P(None, ('tensor', 'section'), 'shard')
- basis_new: bfloat16 [6, 2048, 256], P(None, ('tensor', 'section'))
- moment_m_new: float32 [6, 8192, 256], P(None, ('shard', 'tensor', 'section'))
- moment_v_new: float32 [6, 8192, 256], P(None, ('shard', 'tensor', 'section'))
All inputs are finite; a program needn't handle non-finite values. Where the computation divides by a largest or mean magnitude, that divisor is 1e-20 or more.
Results may differ from a plain program's by a relative error of at most 0.0049.
Values may be sent and summed in bfloat16 or wider, within the bound.
A program may use at most 64 MiB of HBM per device.

v0:
```python
import math
import jax
import jax.numpy as jnp
from jax import lax
from jax.sharding import PartitionSpec as P

D = 2048
NS_ITERS = 4
beta_one = 0.9
beta_two = 0.999
bias_one = 1.0 - 0.9**10
bias_two = 1.0 - 0.999**10
eps_adam = 1e-08
galore_gain = 4.0


def gram_total(iterate):
    local_gram = jnp.einsum("kmr,kms->krs", iterate, iterate, precision=lax.Precision.HIGHEST)
    return lax.psum(local_gram, ("tensor", "section"))


def orthogonal(subspace):
    gram_mat = gram_total(subspace)
    row_bound = jnp.max(jnp.sum(jnp.abs(gram_mat), axis=2), axis=1)[:, None, None] + 1e-06
    iterate = subspace / jnp.sqrt(row_bound)
    gram_mat = gram_mat / row_bound
    identity = jnp.eye(gram_mat.shape[1], dtype=jnp.float32)
    for turn_index in range(NS_ITERS):
        factor = 1.5 * identity - 0.5 * gram_mat
        iterate = jnp.einsum("kmr,krs->kms", iterate, factor, precision=lax.Precision.HIGHEST)
        if turn_index + 1 < NS_ITERS:
            gram_mat = gram_total(iterate)
    return iterate


def per_device(gradient, basis, moment_m, moment_v):
    width_root = math.sqrt(D)
    partial_low = jnp.einsum("kmn,kmr->knr", gradient, basis, preferred_element_type=jnp.float32)
    low_rank = (
        lax.psum_scatter(partial_low, ("tensor", "section"), scatter_dimension=1, tiled=True)
        / width_root
    )
    moment_m_new = beta_one * moment_m + (1.0 - beta_one) * low_rank
    moment_v_new = beta_two * moment_v + (1.0 - beta_two) * low_rank * low_rank
    step_low = (moment_m_new / bias_one / (jnp.sqrt(moment_v_new / bias_two) + eps_adam)).astype(
        jnp.bfloat16
    )
    rough_low = low_rank.astype(jnp.bfloat16)
    step_block, rough_block = (
        lax.all_gather(step_low, ("tensor", "section"), axis=1, tiled=True),
        lax.all_gather(rough_low, ("tensor", "section"), axis=1, tiled=True),
    )
    delta = (
        -galore_gain
        / width_root
        * jnp.einsum("kmr,knr->kmn", basis, step_block, preferred_element_type=jnp.float32)
    ).astype(jnp.bfloat16)
    subspace = jnp.einsum("kmn,knr->kmr", gradient, rough_block, preferred_element_type=jnp.float32)
    whole_sum = lax.psum(subspace, "shard")
    basis_new = (width_root * orthogonal(whole_sum)).astype(jnp.bfloat16)
    return (delta, basis_new, moment_m_new, moment_v_new)


def solution(mesh):
    placed = (
        P(None, ("tensor", "section"), "shard"),
        P(None, ("tensor", "section"), None),
        P(None, ("shard", "tensor", "section"), None),
        P(None, ("shard", "tensor", "section"), None),
    )
    return jax.shard_map(
        per_device,
        mesh=mesh,
        in_specs=placed,
        out_specs=(
            P(None, ("tensor", "section"), "shard"),
            P(None, ("tensor", "section"), None),
            P(None, ("shard", "tensor", "section"), None),
            P(None, ("shard", "tensor", "section"), None),
        ),
        check_vma=False,
    )
```

profile of v0, /device:TPU:32, one launch (start us, length us, event | category | flops | bytes accessed | tf_op | source)
XLA Modules:
  0.0 738.4 jit_solution(1374766177256162602)
XLA Ops:
  7.2 0.0 copy-start
  7.2 0.0 reduce-scatter.2.cloned.1.call-start
  7.2 1.1 copy-done
  8.3 3.3 fusion.37
  11.6 0.0 copy-start.3
  11.6 0.0 copy-start.4
  11.6 0.0 reduce-scatter.2.cloned.1.call-update
  11.6 0.0 all-gather.5.cloned.1.call-start
  11.6 84.4 %reduce-scatter.2.cloned.1.call-done = f32[6,32,256]{2,1,0:T(8,128)} async-done(((f32[6,512,256]{2,1,0:T(8,128)}), f32[6,32,256]{2,1,0:T(8,128)}) %reduce-scatter.2.cloned.1.call-update) | async-done | bytes 196624 | tf_op jit(solution)/shard_map/reduce_scatter | solution.py:40
  96.0 0.0 copy-done.3
  96.0 0.0 copy-done.4
  96.0 1.8 divide_convert_fusion
  97.8 0.0 all-gather.5.cloned.1.call-update
  97.9 0.0 all-reduce.6.cloned.1.call-start
  97.9 49.2 %all-gather.5.cloned.1.call-done = bf16[6,512,256]{2,1,0:T(8,128)(2,1)} async-done(((bf16[6,32,256]{2,1,0:T(8,128)(2,1)}), bf16[6,512,256]{2,1,0:T(8,128)(2,1)}) %all-gather.5.cloned.1.call-update) | async-done | bytes 1572880 | tf_op jit(solution)/shard_map/all_gather | solution.py:51
  147.2 2.9 convolution_bitcast_fusion
  150.1 0.0 all-reduce.6.cloned.1.call-update
  150.1 0.0 all-reduce.8.cloned.1.call-start
  150.2 108.3 %all-reduce.6.cloned.1.call-done = f32[6,128,256]{1,2,0:T(8,128)} async-done(((f32[6,128,256]{1,2,0:T(8,128)}), f32[6,128,256]{1,2,0:T(8,128)}) %all-reduce.6.cloned.1.call-update) | async-done | bytes 786448 | tf_op jit(solution)/shard_map/psum | solution.py:59
  258.5 3.9 fusion.38
  262.4 0.0 copy-start.1
  262.4 0.0 all-reduce.8.cloned.1.call-update
  262.5 0.0 all-reduce.10.cloned.1.call-start
  262.5 102.3 %all-reduce.8.cloned.1.call-done = f32[6,256,256]{2,1,0:T(8,128)} async-done(((f32[6,256,256]{2,1,0:T(8,128)}), f32[6,256,256]{2,1,0:T(8,128)}) %all-reduce.8.cloned.1.call-update) | async-done | bytes 1572880 | tf_op jit(solution)/shard_map/psum | solution.py:19
  364.8 1.7 abs_reduce_fusion
  366.5 0.1 reduce_max.9
  366.6 0.0 copy-done.1
  366.6 3.2 fusion.9
  369.8 2.6 fusion.39
  372.4 0.0 all-reduce.10.cloned.1.call-update
  372.4 0.0 all-reduce.12.cloned.1.call-start
  372.5 98.7 %all-reduce.10.cloned.1.call-done = f32[6,256,256]{2,1,0:T(8,128)} async-done(((f32[6,256,256]{2,1,0:T(8,128)}), f32[6,256,256]{2,1,0:T(8,128)}) %all-reduce.10.cloned.1.call-update) | async-done | bytes 1572880 | tf_op jit(solution)/shard_map/psum | solution.py:19
  471.1 2.6 fusion.6
  473.7 2.6 fusion.40
  476.3 0.0 all-reduce.12.cloned.1.call-update
  476.4 0.0 all-gather.3.cloned.1.call-start
  476.4 0.7 all-gather.3.cloned.1.call-update
  477.1 0.2 all-reduce.14.cloned.1.call-start
  477.3 97.7 %all-reduce.12.cloned.1.call-done = f32[6,256,256]{2,1,0:T(8,128)} async-done(((f32[6,256,256]{2,1,0:T(8,128)}), f32[6,256,256]{2,1,0:T(8,128)}) %all-reduce.12.cloned.1.call-update) | async-done | bytes 1572880 | tf_op jit(solution)/shard_map/psum | solution.py:19
  575.1 2.6 fusion.3
  577.6 2.6 fusion.41
  580.3 0.0 copy-start.2
  580.3 0.0 all-reduce.14.cloned.1.call-update
  580.3 46.1 %all-gather.3.cloned.1.call-done = bf16[6,512,256]{2,1,0:T(8,128)(2,1)} async-done(((bf16[6,32,256]{2,1,0:T(8,128)(2,1)}), bf16[6,512,256]{2,1,0:T(8,128)(2,1)}) %all-gather.3.cloned.1.call-update) | async-done | bytes 1572880 | tf_op jit(solution)/shard_map/all_gather | solution.py:50
  626.4 0.0 copy-done.2
  626.4 2.0 fusion.13
  628.3 1.2 copy.15
  629.5 98.7 %all-reduce.14.cloned.1.call-done = f32[6,256,256]{2,1,0:T(8,128)} async-done(((f32[6,256,256]{2,1,0:T(8,128)}), f32[6,256,256]{2,1,0:T(8,128)}) %all-reduce.14.cloned.1.call-update) | async-done | bytes 1572880 | tf_op jit(solution)/shard_map/psum | solution.py:19
  728.2 3.3 fusion.17
  (2 shorter events, 0.0 us)
Async XLA Ops:
  7.2 1.1 copy-start
  7.2 88.8 %reduce-scatter.2.cloned.1.call-start = ((), (), s32[]{:S(2)}) async-start(), calls=%async_computation.1 | async-start | bytes 3342336 | tf_op jit(solution)/shard_map/reduce_scatter | solution.py:40
  11.6 84.4 %copy-start.3 = (f32[6,32,256]{2,1,0:T(8,128)S(1)}, f32[6,32,256]{2,1,0:T(8,128)}, u32[]{:S(2)}) copy-start(f32[6,32,256]{2,1,0:T(8,128)} %param.6) | copy-start | bytes 589828
  11.6 84.4 %copy-start.4 = (f32[6,32,256]{2,1,0:T(8,128)S(1)}, f32[6,32,256]{2,1,0:T(8,128)}, u32[]{:S(2)}) copy-start(f32[6,32,256]{2,1,0:T(8,128)} %param.7) | copy-start | bytes 589828
  11.6 135.6 %all-gather.5.cloned.1.call-start = ((), (), s32[]{:S(2)}) async-start(), calls=%async_computation.3 | async-start | bytes 1671168 | tf_op jit(solution)/shard_map/all_gather | solution.py:51
  97.9 160.6 %all-reduce.6.cloned.1.call-start = ((), (), s32[]{:S(2)}) async-start(), calls=%async_computation.4 | async-start | bytes 1572864 | tf_op jit(solution)/shard_map/psum | solution.py:59
  150.1 214.7 %all-reduce.8.cloned.1.call-start = ((), (), s32[]{:S(2)}) async-start(), calls=%async_computation.5 | async-start | bytes 3145728 | tf_op jit(solution)/shard_map/psum | solution.py:19
  262.4 104.2 %copy-start.1 = (f32[6,128,256]{1,2,0:T(8,128)S(1)}, f32[6,128,256]{1,2,0:T(8,128)}, u32[]{:S(2)}) copy-start(f32[6,128,256]{1,2,0:T(8,128)} %all-reduce.6.cloned.1.call-done) | copy-start | bytes 2359300
  262.5 208.7 %all-reduce.10.cloned.1.call-start = ((), (), s32[]{:S(2)}) async-start(), calls=%async_computation.6 | async-start | bytes 3145728 | tf_op jit(solution)/shard_map/psum | solution.py:19
  372.4 202.6 %all-reduce.12.cloned.1.call-start = ((), (), s32[]{:S(2)}) async-start(), calls=%async_computation.7 | async-start | bytes 3145728 | tf_op jit(solution)/shard_map/psum | solution.py:19
  476.4 150.0 %all-gather.3.cloned.1.call-start = ((), (), s32[]{:S(2)}) async-start(), calls=%async_computation.2 | async-start | bytes 1671168 | tf_op jit(solution)/shard_map/all_gather | solution.py:50
  477.1 251.1 %all-reduce.14.cloned.1.call-start = ((), (), s32[]{:S(2)}) async-start(), calls=%async_computation.8 | async-start | bytes 3145728 | tf_op jit(solution)/shard_map/psum | solution.py:19
  580.3 46.1 %copy-start.2 = (bf16[6,128,256]{2,1,0:T(8,128)(2,1)S(1)}, bf16[6,128,256]{2,1,0:T(8,128)(2,1)}, u32[]{:S(2)}) copy-start(bf16[6,128,256]{2,1,0:T(8,128)(2,1)} %param.5) | copy-start | bytes 1179652
Sparse Core Ops, SparseCore 0:
  11.7 84.2 reduce-scatter.1
  99.1 48.0 all-gather.4
  150.2 108.2 all-reduce.5
  262.6 102.1 all-reduce.7
  372.6 98.5 all-reduce.9
  476.5 98.5 all-reduce.11
  578.1 48.1 all-gather.2
  629.7 98.5 all-reduce.13
where the time goes:
time: 739 us; the launch traced here: 738 us
  waiting for transfers between devices  686 us (93%)
  matrix products  31.6 us (4%)
  between operations  14.2 us (2%)
    psum x4, waiting for transfers between devices, gram_total(): return lax.psum(local_gram, ('tensor', 'section'))  397 us
    psum x1, waiting for transfers between devices, per_device(): whole_sum = lax.psum(subspace, 'shard')  108 us
    reduce_scatter x1, waiting for transfers between devices, per_device(): lax.psum_scatter(partial_low, ('tensor', 'section'), scatter_dimension=1,...  84.4 us
    all_gather x1, waiting for transfers between devices, per_device(): lax.all_gather(rough_low, ('tensor', 'section'), axis=1, tiled=True)  49.2 us
    all_gather x1, waiting for transfers between devices, per_device(): lax.all_gather(step_low, ('tensor', 'section'), axis=1, tiled=True)  46.1 us
  transfers between devices with their start and end apart: 8, of which 8 were waited for; matrix products, arithmetic and copies ran while one was open for 1% of the time, Pallas kernels for 0%

commit v1 on v0

--- a/solution.py
+++ b/solution.py
@@ -12,6 +12,28 @@
 bias_two = 1.0 - 0.999**10
 eps_adam = 1e-08
 galore_gain = 4.0
+
+
+def laid_out(blocks, dim):
+    blocks = jnp.moveaxis(blocks, 0, dim)
+    shape = blocks.shape
+    return blocks.reshape(*shape[:dim], shape[dim] * shape[dim + 1], *shape[dim + 2 :])
+
+
+def collect(x, axis, dim):
+    size = lax.axis_size(axis)
+    pairs = [(i, (i + 1) % size) for i in range(size)]
+    back = [(b, a) for a, b in pairs]
+    lower, upper = ([], [])
+    for step in range(size - 1):
+        if step % 2 == 0:
+            lower.append(lax.ppermute(lower[-1] if lower else x, axis, pairs))
+        else:
+            upper.append(lax.ppermute(upper[-1] if upper else x, axis, back))
+    blocks = jnp.stack([*lower[::-1], x, *upper])
+    shift = lax.axis_index(axis) - len(lower)
+    blocks = blocks[(jnp.arange(size) - shift) % size]
+    return laid_out(blocks, dim)
 
 
 def gram_total(iterate):
@@ -47,7 +69,7 @@
     )
     rough_low = low_rank.astype(jnp.bfloat16)
     step_block, rough_block = (
-        lax.all_gather(step_low, ("tensor", "section"), axis=1, tiled=True),
+        collect(step_low, ("tensor", "section"), 1),
         lax.all_gather(rough_low, ("tensor", "section"), axis=1, tiled=True),
     )
     delta = (

time: 739 us -> 692 us (0.936)
  waiting for transfers between devices: 686 us -> 586 us
  starting transfers between devices: 0.51 us -> 39.3 us
  local copies, waits for them, and re-layouts: 2.26 us -> 17.9 us
    psum x4, waiting for transfers between devices: 397 us -> 315 us  [gram_total(): return lax.psum(local_gram, ('tensor', 'section'))]
    all_gather x1 -> x0, waiting for transfers between devices: 46.1 us -> none  [per_device(): lax.all_gather(step_low, ('tensor', 'section'), axis=1, tiled=True)]
    ppermute x0 -> x15, starting transfers between devices: none -> 38.8 us  [the longest x7 37.7 us: collect(): upper.append(lax.ppermute(upper[-1] if upper else x, axis, back))]
    ppermute x0 -> x15, waiting for transfers between devices: none -> 29.2 us  [the longest x8 29.2 us: collect(): lower.append(lax.ppermute(lower[-1] if lower else x, axis, pairs))]
    unnamed x11 -> x34, local copies, waits for them, and re-layouts: 2.26 us -> 14.2 us
  transfers between devices with their start and end apart: 8 -> 22, of which waited for: 8 -> 15; matrix products, arithmetic and copies ran while one was open for 1% -> 4% of each run, Pallas kernels for 0% -> 0%
where the time goes in v1:
time: 692 us
  waiting for transfers between devices  586 us (85%)
  starting transfers between devices  39.3 us (6%)
  matrix products  30.1 us (4%)
  local copies, waits for them, and re-layouts  17.9 us (3%)
  between operations  14.3 us (2%)
    psum x4, waiting for transfers between devices, gram_total(): return lax.psum(local_gram, ('tensor', 'section'))  315 us
    psum x1, waiting for transfers between devices, per_device(): whole_sum = lax.psum(subspace, 'shard')  108 us
    reduce_scatter x1, waiting for transfers between devices, per_device(): lax.psum_scatter(partial_low, ('tensor', 'section'), scatter_dimension=1,...  84.3 us
    all_gather x1, waiting for transfers between devices, per_device(): lax.all_gather(rough_low, ('tensor', 'section'), axis=1, tiled=True)  49.3 us
    ppermute x7, starting transfers between devices, collect(): upper.append(lax.ppermute(upper[-1] if upper else x, axis, back))  37.7 us
    ppermute x8, waiting for transfers between devices, collect(): lower.append(lax.ppermute(lower[-1] if lower else x, axis, pairs))  29.2 us
    unnamed x34, local copies, waits for them, and re-layouts  14.2 us
  transfers between devices with their start and end apart: 22, of which 15 were waited for; matrix products, arithmetic and copies ran while one was open for 4% of the time, Pallas kernels for 0%

profile of v1, /device:TPU:32, one launch (start us, length us, event | category | flops | bytes accessed | tf_op | source)
XLA Modules:
  0.0 691.7 jit_solution(11213821798657025995)
XLA Ops:
  7.2 1.1 copy-done
  8.3 3.3 fusion.39
  11.6 0.0 all-gather.2.cloned.1.call-start
  11.6 84.3 %reduce-scatter.2.cloned.1.call-done = f32[6,32,256]{2,1,0:T(8,128)} async-done(((f32[6,512,256]{2,1,0:T(8,128)}), f32[6,32,256]{2,1,0:T(8,128)}) %reduce-scatter.2.cloned.1.call-update) | async-done | bytes 196624 | tf_op jit(solution)/shard_map/reduce_scatter | solution.py:62
  96.0 1.8 divide_convert_fusion
  97.8 0.0 all-reduce.6.cloned.1.call-start
  97.9 49.3 %all-gather.2.cloned.1.call-done = bf16[6,512,256]{2,1,0:T(8,128)(2,1)} async-done(((bf16[6,32,256]{2,1,0:T(8,128)(2,1)}), bf16[6,512,256]{2,1,0:T(8,128)(2,1)}) %all-gather.2.cloned.1.call-update) | async-done | bytes 1572880 | tf_op jit(solution)/shard_map/all_gather | solution.py:73
  147.1 2.9 convolution_bitcast_fusion
  150.1 0.0 all-reduce.8.cloned.1.call-start
  150.1 108.3 %all-reduce.6.cloned.1.call-done = f32[6,128,256]{1,2,0:T(8,128)} async-done(((f32[6,128,256]{1,2,0:T(8,128)}), f32[6,128,256]{1,2,0:T(8,128)}) %all-reduce.6.cloned.1.call-update) | async-done | bytes 786448 | tf_op jit(solution)/shard_map/psum | solution.py:81
  258.5 3.9 fusion.40
  262.4 0.0 all-reduce.10.cloned.1.call-start
  262.5 102.3 %all-reduce.8.cloned.1.call-done = f32[6,256,256]{2,1,0:T(8,128)} async-done(((f32[6,256,256]{2,1,0:T(8,128)}), f32[6,256,256]{2,1,0:T(8,128)}) %all-reduce.8.cloned.1.call-update) | async-done | bytes 1572880 | tf_op jit(solution)/shard_map/psum | solution.py:41
  364.7 1.7 abs_reduce_fusion
  366.4 0.1 reduce_max.9
  366.6 3.2 fusion.9
  369.7 2.6 fusion.41
  372.4 1.1 collective-permute-start
  373.5 6.9 collective-permute-done
  380.4 5.3 collective-permute-start.8
  385.8 3.5 collective-permute-done.1
  389.3 5.3 collective-permute-start.9
  394.6 4.6 collective-permute-done.2
  399.2 5.3 collective-permute-start.10
  404.5 3.4 collective-permute-done.3
  408.0 5.3 collective-permute-start.11
  413.3 3.1 collective-permute-done.4
  416.5 5.3 collective-permute-start.12
  421.8 2.7 collective-permute-done.5
  424.5 5.4 collective-permute-start.13
  429.9 2.5 collective-permute-done.6
  432.4 5.5 collective-permute-start.14
  438.0 2.6 collective-permute-done.7
  440.5 0.6 bitcast_dynamic-update-slice_fusion.15
  441.2 0.6 bitcast_dynamic-update-slice_fusion.14
  441.8 0.6 bitcast_dynamic-update-slice_fusion.13
  442.4 31.3 %all-reduce.10.cloned.1.call-done = f32[6,256,256]{2,1,0:T(8,128)} async-done(((f32[6,256,256]{2,1,0:T(8,128)}), f32[6,256,256]{2,1,0:T(8,128)}) %all-reduce.10.cloned.1.call-update) | async-done | bytes 1572880 | tf_op jit(solution)/shard_map/psum | solution.py:41
  473.8 2.6 fusion.6
  476.3 2.6 fusion.42
  479.0 0.3 all-reduce.14.cloned.1.call-start
  479.2 0.6 copy-done.8
  479.8 0.6 bitcast_dynamic-update-slice_fusion.12
  480.5 0.6 bitcast_dynamic-update-slice_fusion.11
  481.1 0.6 bitcast_dynamic-update-slice_fusion.10
  481.8 0.6 bitcast_dynamic-update-slice_fusion.9
  482.4 0.6 bitcast_dynamic-update-slice_fusion.8
  483.0 0.6 bitcast_dynamic-update-slice_fusion.7
  483.7 0.6 bitcast_dynamic-update-slice_fusion.6
  484.3 93.4 %all-reduce.12.cloned.1.call-done = f32[6,256,256]{2,1,0:T(8,128)} async-done(((f32[6,256,256]{2,1,0:T(8,128)}), f32[6,256,256]{2,1,0:T(8,128)}) %all-reduce.12.cloned.1.call-update) | async-done | bytes 1572880 | tf_op jit(solution)/shard_map/psum | solution.py:41
  577.7 2.6 fusion.3
  580.2 2.6 fusion.43
  582.9 0.6 bitcast_dynamic-update-slice_fusion.5
  583.5 0.6 bitcast_dynamic-update-slice_fusion.4
  584.1 0.6 bitcast_dynamic-update-slice_fusion.3
  584.8 0.6 bitcast_dynamic-update-slice_fusion.2
  585.4 1.5 bitcast_dynamic-update-slice_fusion.1
  587.0 1.5 bitcast_dynamic-update-slice_fusion
  588.5 2.1 gather_fusion
  590.6 0.1 copy.18
  590.7 0.8 copy-done.2
  591.6 0.6 fusion.13
  592.1 1.2 copy.24
  593.3 88.3 %all-reduce.14.cloned.1.call-done = f32[6,256,256]{2,1,0:T(8,128)} async-done(((f32[6,256,256]{2,1,0:T(8,128)}), f32[6,256,256]{2,1,0:T(8,128)}) %all-reduce.14.cloned.1.call-update) | async-done | bytes 1572880 | tf_op jit(solution)/shard_map/psum | solution.py:41
  681.6 3.3 fusion.17
  (42 shorter events, 0.3 us)
Async XLA Ops:
  7.2 1.1 copy-start
  7.2 88.8 %reduce-scatter.2.cloned.1.call-start = ((), (), s32[]{:S(2)}) async-start(), calls=%async_computation.1 | async-start | bytes 3342336 | tf_op jit(solution)/shard_map/reduce_scatter | solution.py:62
  11.6 84.4 %copy-start.3 = (f32[6,32,256]{2,1,0:T(8,128)S(1)}, f32[6,32,256]{2,1,0:T(8,128)}, u32[]{:S(2)}) copy-start(f32[6,32,256]{2,1,0:T(8,128)} %param.6) | copy-start | bytes 589828
  11.6 84.4 %copy-start.4 = (f32[6,32,256]{2,1,0:T(8,128)S(1)}, f32[6,32,256]{2,1,0:T(8,128)}, u32[]{:S(2)}) copy-start(f32[6,32,256]{2,1,0:T(8,128)} %param.7) | copy-start | bytes 589828
  11.6 135.5 %all-gather.2.cloned.1.call-start = ((), (), s32[]{:S(2)}) async-start(), calls=%async_computation.2 | async-start | bytes 1671168 | tf_op jit(solution)/shard_map/all_gather | solution.py:73
  97.8 160.7 %all-reduce.6.cloned.1.call-start = ((), (), s32[]{:S(2)}) async-start(), calls=%async_computation.3 | async-start | bytes 1572864 | tf_op jit(solution)/shard_map/psum | solution.py:81
  150.1 214.7 %all-reduce.8.cloned.1.call-start = ((), (), s32[]{:S(2)}) async-start(), calls=%async_computation.4 | async-start | bytes 3145728 | tf_op jit(solution)/shard_map/psum | solution.py:41
  262.4 104.2 %copy-start.1 = (f32[6,128,256]{1,2,0:T(8,128)S(1)}, f32[6,128,256]{1,2,0:T(8,128)}, u32[]{:S(2)}) copy-start(f32[6,128,256]{1,2,0:T(8,128)} %all-reduce.6.cloned.1.call-done) | copy-start | bytes 2359300
  262.4 211.4 %all-reduce.10.cloned.1.call-start = ((), (), s32[]{:S(2)}) async-start(), calls=%async_computation.5 | async-start | bytes 3145728 | tf_op jit(solution)/shard_map/psum | solution.py:41
  372.4 205.3 %all-reduce.12.cloned.1.call-start = ((), (), s32[]{:S(2)}) async-start(), calls=%async_computation.6 | async-start | bytes 3145728 | tf_op jit(solution)/shard_map/psum | solution.py:41
  372.4 8.0 %collective-permute-start = (bf16[6,32,256]{2,1,0:T(8,128)(2,1)S(1)}, bf16[6,32,256]{2,1,0:T(8,128)(2,1)S(1)}, u32[]{:S(2)}, u32[]{:S(2)}) collective-permute-start(bf16[6,32,256]{2,1,0:T(8,128)(2,1)S(1)} %get-tuple-element.16), channel_id=1, source_target_pairs={{0,1},{1,2},{2,3},{3,4},{4,5},{5,6},{6,7},{7,8},{8,9},{9,10},{10,1... | collective-permute-start | bytes 294920 | tf_op jit(solution)/shard_map/ppermute | solution.py:30
  380.4 8.9 %collective-permute-start.1 = (bf16[6,32,256]{2,1,0:T(8,128)(2,1)S(1)}, bf16[6,32,256]{2,1,0:T(8,128)(2,1)S(1)}, u32[]{:S(2)}, u32[]{:S(2)}) collective-permute-start(bf16[6,32,256]{2,1,0:T(8,128)(2,1)S(1)} %collective-permute-done), channel_id=1, source_target_pairs={{0,1},{1,2},{2,3},{3,4},{4,5},{5,6},{6,7},{7,8},{8,9},{9,10},{10,1... | collective-permute-start | bytes 294920 | tf_op jit(solution)/shard_map/ppermute | solution.py:30
  380.4 8.9 %collective-permute-start.8 = (bf16[6,32,256]{2,1,0:T(8,128)(2,1)S(1)}, bf16[6,32,256]{2,1,0:T(8,128)(2,1)S(1)}, u32[]{:S(2)}, u32[]{:S(2)}) collective-permute-start(bf16[6,32,256]{2,1,0:T(8,128)(2,1)S(1)} %get-tuple-element.16), channel_id=1, source_target_pairs={{1,0},{2,1},{3,2},{4,3},{5,4},{6,5},{7,6},{8,7},{9,8},{10,9},{11,1... | collective-permute-start | bytes 294920 | tf_op jit(solution)/shard_map/ppermute | solution.py:32
  389.3 9.9 %collective-permute-start.2 = (bf16[6,32,256]{2,1,0:T(8,128)(2,1)S(1)}, bf16[6,32,256]{2,1,0:T(8,128)(2,1)S(1)}, u32[]{:S(2)}, u32[]{:S(2)}) collective-permute-start(bf16[6,32,256]{2,1,0:T(8,128)(2,1)S(1)} %collective-permute-done.1), channel_id=1, source_target_pairs={{0,1},{1,2},{2,3},{3,4},{4,5},{5,6},{6,7},{7,8},{8,9},{9,10},{10,1... | collective-permute-start | bytes 294920 | tf_op jit(solution)/shard_map/ppermute | solution.py:30
  389.3 9.9 %collective-permute-start.9 = (bf16[6,32,256]{2,1,0:T(8,128)(2,1)S(1)}, bf16[6,32,256]{2,1,0:T(8,128)(2,1)S(1)}, u32[]{:S(2)}, u32[]{:S(2)}) collective-permute-start(bf16[6,32,256]{2,1,0:T(8,128)(2,1)S(1)} %collective-permute-done.8), channel_id=1, source_target_pairs={{1,0},{2,1},{3,2},{4,3},{5,4},{6,5},{7,6},{8,7},{9,8},{10,9},{11,1... | collective-permute-start | bytes 294920 | tf_op jit(solution)/shard_map/ppermute | solution.py:32
  399.2 8.8 %collective-permute-start.3 = (bf16[6,32,256]{2,1,0:T(8,128)(2,1)S(1)}, bf16[6,32,256]{2,1,0:T(8,128)(2,1)S(1)}, u32[]{:S(2)}, u32[]{:S(2)}) collective-permute-start(bf16[6,32,256]{2,1,0:T(8,128)(2,1)S(1)} %collective-permute-done.2), channel_id=1, source_target_pairs={{0,1},{1,2},{2,3},{3,4},{4,5},{5,6},{6,7},{7,8},{8,9},{9,10},{10,1... | collective-permute-start | bytes 294920 | tf_op jit(solution)/shard_map/ppermute | solution.py:30
  399.2 8.8 %collective-permute-start.10 = (bf16[6,32,256]{2,1,0:T(8,128)(2,1)S(1)}, bf16[6,32,256]{2,1,0:T(8,128)(2,1)S(1)}, u32[]{:S(2)}, u32[]{:S(2)}) collective-permute-start(bf16[6,32,256]{2,1,0:T(8,128)(2,1)S(1)} %collective-permute-done.9), channel_id=1, source_target_pairs={{1,0},{2,1},{3,2},{4,3},{5,4},{6,5},{7,6},{8,7},{9,8},{10,9},{11,1... | collective-permute-start | bytes 294920 | tf_op jit(solution)/shard_map/ppermute | solution.py:32
  408.0 8.5 %collective-permute-start.4 = (bf16[6,32,256]{2,1,0:T(8,128)(2,1)S(1)}, bf16[6,32,256]{2,1,0:T(8,128)(2,1)S(1)}, u32[]{:S(2)}, u32[]{:S(2)}) collective-permute-start(bf16[6,32,256]{2,1,0:T(8,128)(2,1)S(1)} %collective-permute-done.3), channel_id=1, source_target_pairs={{0,1},{1,2},{2,3},{3,4},{4,5},{5,6},{6,7},{7,8},{8,9},{9,10},{10,1... | collective-permute-start | bytes 294920 | tf_op jit(solution)/shard_map/ppermute | solution.py:30
  408.0 8.5 %collective-permute-start.11 = (bf16[6,32,256]{2,1,0:T(8,128)(2,1)S(1)}, bf16[6,32,256]{2,1,0:T(8,128)(2,1)S(1)}, u32[]{:S(2)}, u32[]{:S(2)}) collective-permute-start(bf16[6,32,256]{2,1,0:T(8,128)(2,1)S(1)} %collective-permute-done.10), channel_id=1, source_target_pairs={{1,0},{2,1},{3,2},{4,3},{5,4},{6,5},{7,6},{8,7},{9,8},{10,9},{11,1... | collective-permute-start | bytes 294920 | tf_op jit(solution)/shard_map/ppermute | solution.py:32
  416.5 26.0 %copy-start.7 = (bf16[6,32,256]{2,1,0:T(8,128)(2,1)}, bf16[6,32,256]{2,1,0:T(8,128)(2,1)S(1)}, u32[]{:S(2)}) copy-start(bf16[6,32,256]{2,1,0:T(8,128)(2,1)S(1)} %collective-permute-done.4) | copy-start | bytes 294916
  416.5 8.0 %collective-permute-start.5 = (bf16[6,32,256]{2,1,0:T(8,128)(2,1)S(1)}, bf16[6,32,256]{2,1,0:T(8,128)(2,1)S(1)}, u32[]{:S(2)}, u32[]{:S(2)}) collective-permute-start(bf16[6,32,256]{2,1,0:T(8,128)(2,1)S(1)} %collective-permute-done.4), channel_id=1, source_target_pairs={{0,1},{1,2},{2,3},{3,4},{4,5},{5,6},{6,7},{7,8},{8,9},{9,10},{10,1... | collective-permute-start | bytes 294920 | tf_op jit(solution)/shard_map/ppermute | solution.py:30
  416.5 8.0 %collective-permute-start.12 = (bf16[6,32,256]{2,1,0:T(8,128)(2,1)S(1)}, bf16[6,32,256]{2,1,0:T(8,128)(2,1)S(1)}, u32[]{:S(2)}, u32[]{:S(2)}) collective-permute-start(bf16[6,32,256]{2,1,0:T(8,128)(2,1)S(1)} %collective-permute-done.11), channel_id=1, source_target_pairs={{1,0},{2,1},{3,2},{4,3},{5,4},{6,5},{7,6},{8,7},{9,8},{10,9},{11,1... | collective-permute-start | bytes 294920 | tf_op jit(solution)/shard_map/ppermute | solution.py:32
  424.5 7.9 %collective-permute-start.6 = (bf16[6,32,256]{2,1,0:T(8,128)(2,1)S(1)}, bf16[6,32,256]{2,1,0:T(8,128)(2,1)S(1)}, u32[]{:S(2)}, u32[]{:S(2)}) collective-permute-start(bf16[6,32,256]{2,1,0:T(8,128)(2,1)S(1)} %collective-permute-done.5), channel_id=1, source_target_pairs={{0,1},{1,2},{2,3},{3,4},{4,5},{5,6},{6,7},{7,8},{8,9},{9,10},{10,1... | collective-permute-start | bytes 294920 | tf_op jit(solution)/shard_map/ppermute | solution.py:30
  424.5 18.0 %copy-start.5 = (bf16[6,32,256]{2,1,0:T(8,128)(2,1)}, bf16[6,32,256]{2,1,0:T(8,128)(2,1)S(1)}, u32[]{:S(2)}) copy-start(bf16[6,32,256]{2,1,0:T(8,128)(2,1)S(1)} %collective-permute-done.12) | copy-start | bytes 294916
  424.5 7.9 %collective-permute-start.13 = (bf16[6,32,256]{2,1,0:T(8,128)(2,1)S(1)}, bf16[6,32,256]{2,1,0:T(8,128)(2,1)}, u32[]{:S(2)}, u32[]{:S(2)}) collective-permute-start(bf16[6,32,256]{2,1,0:T(8,128)(2,1)S(1)} %collective-permute-done.12), channel_id=1, source_target_pairs={{1,0},{2,1},{3,2},{4,3},{5,4},{6,5},{7,6},{8,7},{9,8},{10,9},{11,1... | collective-permute-start | bytes 294920 | tf_op jit(solution)/shard_map/ppermute | solution.py:32
  432.4 8.1 %collective-permute-start.7 = (bf16[6,32,256]{2,1,0:T(8,128)(2,1)S(1)}, bf16[6,32,256]{2,1,0:T(8,128)(2,1)S(1)}, u32[]{:S(2)}, u32[]{:S(2)}) collective-permute-start(bf16[6,32,256]{2,1,0:T(8,128)(2,1)S(1)} %collective-permute-done.6), channel_id=1, source_target_pairs={{0,1},{1,2},{2,3},{3,4},{4,5},{5,6},{6,7},{7,8},{8,9},{9,10},{10,1... | collective-permute-start | bytes 294920 | tf_op jit(solution)/shard_map/ppermute | solution.py:30
  432.4 154.5 %collective-permute-start.14 = (bf16[6,32,256]{2,1,0:T(8,128)(2,1)}, bf16[6,32,256]{2,1,0:T(8,128)(2,1)}, u32[]{:S(2)}, u32[]{:S(2)}) collective-permute-start(bf16[6,32,256]{2,1,0:T(8,128)(2,1)} %collective-permute-done.13), channel_id=1, source_target_pairs={{1,0},{2,1},{3,2},{4,3},{5,4},{6,5},{7,6},{8,7},{9,8},{10,9},{11,1... | collective-permute-start | bytes 294920 | tf_op jit(solution)/shard_map/ppermute | solution.py:32
  478.9 0.9 copy-start.8
  479.0 202.6 %all-reduce.14.cloned.1.call-start = ((), (), s32[]{:S(2)}) async-start(), calls=%async_computation.7 | async-start | bytes 3145728 | tf_op jit(solution)/shard_map/psum | solution.py:41
  582.8 2.0 copy-start.6
  590.6 1.0 copy-start.2
Sparse Core Ops, SparseCore 0:
  11.7 84.2 reduce-scatter.1
  99.0 48.0 all-gather.1
  150.2 108.2 all-reduce.5
  262.5 102.1 all-reduce.7
  372.5 101.2 all-reduce.9
  479.1 98.5 all-reduce.11
  583.0 98.5 all-reduce.13
